TPU v7x, 256 devices: a whole 4x4x8 slice. The times are simulated.
256 devices in a mesh: dp: 64 (over x, z, core), mp: 4 (over y).
Axes of the slice: x: 4, y: 4, z: 8, core: 2. Of those that a mesh axis runs over, the one named last changes fastest.
Arguments:
- history: bfloat16 [1024, 32, 1024], P('dp', None, 'mp'), may hold values from -6 to 6
- lengths: int32 [1024], replicated, may hold values from 1 to 32, 16384 in all
- source: int32 [1024], replicated, may hold values from 0 to 1023, as said below
- owners: int32 [32768, 8], P(('dp', 'mp')), may hold values from 0 to 255, all different within a row; in each aligned block of 128 rows (0 to 127, 128 to 255, ...) at most 6 rows name the same one
- item_rows: int32 [32768, 8], P(('dp', 'mp')), may hold values from 0 to 511
- catalogue: bfloat16 [131072, 1024], P(('dp', 'mp')), may hold values from -6 to 6
- w_in: bfloat16 [4, 1024, 1024], P(None, None, 'mp'), may hold values from -0.1875 to 0.1875
- w_out: bfloat16 [1024, 1024], P('mp'), may hold values from -0.1875 to 0.1875
Outputs:
- w_in_grad: float32 [4, 1024, 1024], P(None, 'dp', 'mp')
- w_out_grad: float32 [1024, 1024], P('mp', 'dp')
- cat_grad: float32 [131072, 1024], P(('dp', 'mp'))
Inputs may be any that keep to these rules, and one draw needn't show every extreme that they name: `source`: a permutation; balanced slot k lies on index k // 16 of dp, and the 16 histories that start on one index of dp go to one index of dp at most (16 + 64 - 1) // 64 at a time, that many for some index. Each event names 8 different owners, column 0 the positive item's; the events of one device (aligned blocks of 128) name one owner at most 6 times.
All inputs are finite; a program needn't handle non-finite values.
Results may differ from a plain program's by a relative error of at most 0.017.
Values may be sent and summed in bfloat16 or wider, within the bound.
A program may use at most 128 MiB of HBM per device.

v0:
```python
import jax
import jax.numpy as jnp
from jax import lax
from jax.sharding import PartitionSpec as P

DH = 128
cosine_divisor = 0.05
epsilon_norm = 1e-05
epsilon_unit = 1e-06


def normalize(rows_in):
    centered = rows_in - jnp.mean(rows_in, axis=-1, keepdims=True)
    spread = jnp.mean(centered * centered, axis=-1, keepdims=True)
    return centered / jnp.sqrt(spread + epsilon_norm)


def attend(projected, length_here):
    gating = projected[0]
    values = projected[1]
    queries = projected[2]
    key_rows = projected[3]
    steps_n = projected.shape[1]
    scores = jnp.einsum(
        "thd,shd->hts", queries, key_rows, preferred_element_type=jnp.float32
    ) / jnp.sqrt(jnp.float32(projected.shape[3]))
    places = jnp.arange(steps_n, dtype=jnp.int32)
    allowed = (places[None, :] <= places[:, None]) & (places[None, :] < length_here)
    weights = jnp.where(
        allowed[None], jax.nn.silu(scores) / length_here.astype(jnp.float32), 0.0
    ).astype(jnp.bfloat16)
    mixed_out = jnp.einsum("hts,shd->thd", weights, values, preferred_element_type=jnp.float32)
    return (normalize(mixed_out) * gating.astype(jnp.float32)).astype(jnp.bfloat16)


def loss_block(out_rows, valid_rows, fetched):
    out_norm = jnp.sqrt(jnp.sum(out_rows * out_rows, axis=-1, keepdims=True) + epsilon_unit)
    request_unit_vector = out_rows / out_norm
    item_f = fetched.astype(jnp.float32)
    item_norm = jnp.sqrt(jnp.sum(item_f * item_f, axis=-1, keepdims=True) + epsilon_unit)
    catalog_unit_vector = item_f / item_norm
    cosine_match_raw = (
        jnp.einsum("qn,qgn->qg", request_unit_vector, catalog_unit_vector) / cosine_divisor
    )
    expo = jnp.exp(cosine_match_raw)
    probs = expo / jnp.sum(expo, axis=-1, keepdims=True)
    column = jnp.arange(cosine_match_raw.shape[1], dtype=jnp.int32)
    exponent_shares = (probs - (column[None, :] == 0).astype(jnp.float32)) * valid_rows[
        :, None
    ].astype(jnp.float32)
    request_unit_vector_slope = (
        jnp.einsum("as,asy->ay", exponent_shares, catalog_unit_vector) / cosine_divisor
    )
    out_grad = (
        request_unit_vector_slope
        - request_unit_vector
        * jnp.sum(request_unit_vector * request_unit_vector_slope, axis=-1, keepdims=True)
    ) / out_norm
    catalog_unit_vector_slope = (
        exponent_shares[:, :, None] * request_unit_vector[:, None, :] / cosine_divisor
    )
    item_grad = (
        catalog_unit_vector_slope
        - catalog_unit_vector
        * jnp.sum(catalog_unit_vector * catalog_unit_vector_slope, axis=-1, keepdims=True)
    ) / item_norm
    return (out_grad, item_grad)


def silu_slope(preact):
    sigma = jax.nn.sigmoid(preact)
    return sigma * (1.0 + preact * (1.0 - sigma))


def earlier_same(labels):
    order_ids = jnp.arange(labels.shape[0], dtype=jnp.int32)
    same = (labels[None, :] == labels[:, None]) & (order_ids[None, :] < order_ids[:, None])
    return jnp.sum(same.astype(jnp.int32), axis=1)


def per_device(history, lengths, source, owners, item_rows, catalogue, w_in, w_out):
    dp_count = lax.axis_size("dp")
    mp_count = lax.axis_size("mp")
    dev_count = dp_count * mp_count
    here_dp = lax.axis_index("dp")
    here_mp = lax.axis_index("mp")
    seq_dev, steps_n, cols_here = history.shape
    seq_total = source.shape[0]
    per_peer = (seq_dev + dp_count - 1) // dp_count
    target = (
        jnp.zeros((seq_total,), jnp.int32).at[source].set(jnp.arange(seq_total, dtype=jnp.int32))
    )
    slot_ids = jnp.arange(seq_dev, dtype=jnp.int32)
    my_seqs = here_dp * seq_dev + slot_ids
    dest_dev = target[my_seqs] // seq_dev
    send_rank = earlier_same(dest_dev)
    outgoing = (
        jnp.zeros((dp_count, per_peer, steps_n, cols_here), jnp.bfloat16)
        .at[dest_dev, send_rank]
        .set(history)
    )
    arrived = lax.all_to_all(outgoing, "dp", split_axis=0, concat_axis=0, tiled=True)
    taken = source[my_seqs]
    anchor = taken // seq_dev
    anchor_block = anchor[:, None] * seq_dev + slot_ids[None, :]
    goes_here = target[anchor_block] // seq_dev == here_dp
    earlier = slot_ids[None, :] < (taken % seq_dev)[:, None]
    recv_rank = jnp.sum((goes_here & earlier).astype(jnp.int32), axis=1)
    counts = lengths[taken]
    local_rows = jnp.take(
        arrived.reshape(dp_count * per_peer, steps_n, cols_here),
        anchor * per_peer + recv_rank,
        axis=0,
    )
    features = lax.all_gather(local_rows, "mp", axis=2, tiled=True)
    rows_all = seq_dev * steps_n
    width = features.shape[2]
    flat_rows = features.reshape(rows_all, width)
    normed = normalize(flat_rows.astype(jnp.float32)).astype(jnp.bfloat16)
    preact = jnp.einsum("rd,cdh->crh", normed, w_in, preferred_element_type=jnp.float32)
    projected = jax.nn.silu(preact).astype(jnp.bfloat16)
    cols_heads = w_in.shape[2]
    heads_here = cols_heads // DH
    grouped = projected.reshape(4, seq_dev, steps_n, heads_here, DH)

    def run_all(inputs):
        return jax.vmap(attend, in_axes=(1, 0))(inputs, counts)

    gated, back = jax.vjp(run_all, grouped)
    gated_flat = gated.reshape(rows_all, cols_heads)
    partial_out = jnp.dot(gated_flat, w_out, preferred_element_type=jnp.float32)
    quarter = rows_all // mp_count
    summed = lax.psum(partial_out, "mp")
    out_rows = lax.dynamic_slice_in_dim(summed, here_mp * quarter, quarter, 0)
    out_rows = out_rows + lax.dynamic_slice_in_dim(flat_rows, here_mp * quarter, quarter, 0).astype(
        jnp.float32
    )
    position = here_mp * quarter + jnp.arange(quarter, dtype=jnp.int32)
    valid_rows = position % steps_n < counts[position // steps_n]
    top_n = owners.shape[1]
    asks = quarter * top_n
    capacity = max(2, (3 * asks + 2 * dev_count - 1) // (2 * dev_count))
    owner_flat = owners.reshape(-1)
    row_flat = item_rows.reshape(-1)
    rank_in = earlier_same(owner_flat)
    address = owner_flat * capacity + rank_in
    slot_table = (
        jnp.full((dev_count * capacity,), asks, jnp.int32)
        .at[address]
        .set(jnp.arange(asks, dtype=jnp.int32))
    )
    is_used = slot_table < asks
    safe_index = jnp.minimum(slot_table, asks - 1)
    wanted = jnp.where(is_used, row_flat[safe_index], 0).reshape(dp_count, mp_count, capacity)
    incoming = lax.all_to_all(
        lax.all_to_all(wanted, "dp", split_axis=0, concat_axis=0, tiled=True),
        "mp",
        split_axis=1,
        concat_axis=1,
        tiled=True,
    )
    incoming_flat = incoming.reshape(-1)
    looked = jnp.take(catalogue, incoming_flat, axis=0).reshape(dp_count, mp_count, capacity, width)
    returned = lax.all_to_all(
        lax.all_to_all(looked, "dp", split_axis=0, concat_axis=0, tiled=True),
        "mp",
        split_axis=1,
        concat_axis=1,
        tiled=True,
    )
    fetched = jnp.take(returned.reshape(dev_count * capacity, width), address, axis=0).reshape(
        quarter, top_n, width
    )
    out_grad, item_grad = loss_block(out_rows, valid_rows, fetched)
    item_flat = item_grad.reshape(asks, width)
    sending = jnp.where(is_used[:, None], jnp.take(item_flat, safe_index, axis=0), 0.0)
    landed = lax.all_to_all(
        lax.all_to_all(
            sending.reshape(dp_count, mp_count, capacity, width).astype(jnp.bfloat16),
            "dp",
            split_axis=0,
            concat_axis=0,
            tiled=True,
        ),
        "mp",
        split_axis=1,
        concat_axis=1,
        tiled=True,
    ).astype(jnp.float32)
    cat_grad = (
        jnp.zeros((catalogue.shape[0], width), jnp.float32)
        .at[incoming_flat]
        .add(landed.reshape(-1, width))
    )
    out_cotangent = lax.all_gather(out_grad.astype(jnp.bfloat16), "mp", axis=0, tiled=True)
    w_out_part = jnp.einsum(
        "rh,rd->hd", gated_flat, out_cotangent, preferred_element_type=jnp.float32
    )
    gated_cotangent = jnp.einsum(
        "rd,hd->rh", out_cotangent, w_out, preferred_element_type=jnp.float32
    ).astype(jnp.bfloat16)
    (grouped_cotangent,) = back(gated_cotangent.reshape(seq_dev, steps_n, heads_here, DH))
    projected_cotangent = grouped_cotangent.reshape(4, rows_all, cols_heads)
    preact_cotangent = (projected_cotangent.astype(jnp.float32) * silu_slope(preact)).astype(
        jnp.bfloat16
    )
    w_in_part = jnp.einsum(
        "rd,crh->cdh", normed, preact_cotangent, preferred_element_type=jnp.float32
    )
    w_in_grad, w_out_grad = (
        lax.psum_scatter(w_in_part, "dp", scatter_dimension=1, tiled=True),
        lax.psum_scatter(w_out_part, "dp", scatter_dimension=1, tiled=True),
    )
    return (w_in_grad, w_out_grad, cat_grad)


def solution(mesh):
    placed = (
        P("dp", None, "mp"),
        P(),
        P(),
        P(("dp", "mp"), None),
        P(("dp", "mp"), None),
        P(("dp", "mp"), None),
        P(None, None, "mp"),
        P("mp", None),
    )
    return jax.shard_map(
        per_device,
        mesh=mesh,
        in_specs=placed,
        out_specs=(P(None, "dp", "mp"), P("mp", "dp"), P(("dp", "mp"), None)),
        check_vma=False,
    )
```

profile of v0, /device:TPU:8, one launch (start us, length us, event | category | flops | bytes accessed | tf_op | source)
XLA Modules:
  0.0 688.2 jit_solution(856039338225278554)
XLA Ops:
  15.3 5.9 gather_fusion.5
  22.6 11.9 %all-to-all-start.1 = ((s32[64,4,6]{2,1,0:T(4,128)}), s32[64,4,6]{2,1,0:T(4,128)S(1)}, u32[]{:S(2)}, u32[]{:S(2)}) async-start(s32[64,4,6]{2,1,0:T(4,128)} %reshape.655), calls=%async_computation.1 | async-start | bytes 262144 | tf_op jit(solution)/shard_map/all_to_all | solution.py:156
  40.4 4.4 all-to-all-done.1
  45.6 4.9 all-to-all-start.2
  54.4 6.4 all-to-all-start
  62.7 5.8 gather_fusion.6
  68.6 6.2 gather.53
  77.4 7.9 %copy.116 = bf16[64,4,6,1024]{3,1,2,0:T(4,128)(2,1)} copy(bf16[64,4,6,1024]{3,2,1,0:T(8,128)(2,1)S(1)} %broadcast_select_fusion) | data formatting | bytes 6291456 | tf_op jit(solution)/shard_map/jit(_take)/select_n | solution.py:163
  88.8 7.2 %all-to-all-start.3 = ((bf16[64,4,6,1024]{3,1,2,0:T(4,128)(2,1)}), bf16[64,4,6,1024]{3,1,2,0:T(4,128)(2,1)}, u32[]{:S(2)}, u32[]{:S(2)}) async-start(bf16[64,4,6,1024]{3,1,2,0:T(4,128)(2,1)} %copy.116), calls=%async_computation.3 | async-start | bytes 6291456 | tf_op jit(solution)/shard_map/all_to_all | solution.py:165
  101.8 27.1 %all-gather.3.cloned.1.call-done = bf16[16,32,1024]{2,1,0:T(8,128)(2,1)} async-done(((bf16[16,32,256]{2,1,0:T(8,128)(2,1)}), bf16[16,32,1024]{2,1,0:T(8,128)(2,1)}) %all-gather.3.cloned.1.call-update) | async-done | bytes 1048592 | tf_op jit(solution)/shard_map/all_gather | solution.py:115
  140.8 27.9 %all-to-all-done.3 = bf16[64,4,6,1024]{3,1,2,0:T(4,128)(2,1)} async-done(((bf16[64,4,6,1024]{3,1,2,0:T(4,128)(2,1)}), bf16[64,4,6,1024]{3,1,2,0:T(4,128)(2,1)}, u32[]{:S(2)}, u32[]{:S(2)}) %all-to-all-start.3) | async-done | bytes 3145760 | tf_op jit(solution)/shard_map/all_to_all | solution.py:165
  168.6 5.3 copy.117
  173.9 5.4 all-to-all-start.4
  185.5 10.0 %compare_convert_fusion = f32[128]{0:T(128)S(1)} fusion(s32[]{:T(128)} %bitcast.39, s32[]{:T(128)} %bitcast.40, s32[]{:T(128)} %bitcast.41, s32[]{:T(128)} %bitcast.42, s32[]{:T(128)} %bitcast.43, s32[]{:T(128)} %bitcast.45, s32[]{:T(128)} %bitcast.44, s32[]{:T(128)} %bitcast.22, s32[]{:T(128)} %bitcast.24, s32[]{:T(128)} %bitcast.26, s32[]{:T(128)} %bitcast.28, ...), kind=kLoop, calls=%fused_computation.196 | loop fusion | flops 8064 | bytes 580 | tf_op jit(solution)/shard_map/convert_element_type | solution.py:50
  196.8 34.2 %all-reduce.8.cloned.1.call-done = f32[512,1024]{1,0:T(8,128)} async-done(((f32[512,1024]{1,0:T(8,128)}), f32[512,1024]{1,0:T(8,128)}) %all-reduce.8.cloned.1.call-update) | async-done | bytes 2097168 | tf_op jit(solution)/shard_map/psum | solution.py:133
  238.1 4.9 reshape.657
  243.0 5.3 gather_fusion.7
  259.0 5.8 gather_fusion.8
  264.8 6.2 gather.58
  271.1 4.7 fusion.1
  279.9 5.8 all-to-all-start.5
  286.9 28.9 %all-gather.5.cloned.1.call-done = bf16[512,1024]{1,0:T(8,128)(2,1)} async-done(((bf16[128,1024]{1,0:T(8,128)(2,1)}), bf16[512,1024]{1,0:T(8,128)(2,1)}) %all-gather.5.cloned.1.call-update) | async-done | bytes 1048592 | tf_op jit(solution)/shard_map/all_gather | solution.py:195
  326.0 6.1 convolution_bitcast_fusion
  332.2 5.2 copy.129
  337.4 21.5 %all-to-all-done.5 = bf16[64,4,6,1024]{3,1,2,0:T(4,128)(2,1)} async-done(((bf16[64,4,6,1024]{3,1,2,0:T(4,128)(2,1)}), bf16[64,4,6,1024]{3,1,2,0:T(4,128)(2,1)}, u32[]{:S(2)}, u32[]{:S(2)}) %all-to-all-start.5) | async-done | bytes 3145760 | tf_op jit(solution)/shard_map/all_to_all | solution.py:178
  358.9 5.4 copy.134
  364.3 6.6 all-to-all-start.6
  375.0 163.0 %all-reduce.10.cloned.1.call-done = f32[4,1024,256]{2,0,1:T(4,128)} async-done(((f32[4,1024,256]{2,0,1:T(4,128)}), f32[4,1024,256]{2,0,1:T(4,128)}) %all-reduce.10.cloned.1.call-update) | async-done | bytes 4194320
  539.4 5.1 copy.135
  544.6 8.4 %reshape.790 = f32[1536,1024]{1,0:T(8,128)} reshape(f32[64,4,6,1024]{3,2,1,0:T(8,128)} %copy.135) | data formatting | bytes 12582912 | tf_op jit(solution)/shard_map/reshape | solution.py:193
  553.0 16.1 %scatter_custom_fusion.3 = f32[512,1024]{1,0:T(8,128)} fusion(s32[1536]{0:T(1024)} %copy-done.39, f32[1536,1024]{1,0:T(8,128)} %reshape.790, f32[]{:T(128)} %constant.182.clone.1), kind=kCustom, calls=%fused_computation.68 | custom fusion | flops 1572864 | bytes 2097664 | tf_op jit(solution)/shard_map/scatter-add | solution.py:193
  569.1 112.4 %reduce-scatter.2.cloned.1.call-done = f32[256,16]{0,1:T(8,128)} async-done(((f32[256,1024]{0,1:T(8,128)}), f32[256,16]{0,1:T(8,128)}) %reduce-scatter.2.cloned.1.call-update) | async-done | bytes 16400 | tf_op jit(solution)/shard_map/reduce_scatter | solution.py:212
  (235 shorter events, 90.7 us)
Async XLA Ops:
  7.2 125.0 %copy-start = (bf16[4,1024,256]{2,1,0:T(8,128)(2,1)S(1)}, bf16[4,1024,256]{2,1,0:T(8,128)(2,1)}, u32[]{:S(2)}) copy-start(bf16[4,1024,256]{2,1,0:T(8,128)(2,1)} %param.14) | copy-start | bytes 6291460
  9.3 5.1 copy-start.38
  14.4 6.8 copy-start.29
  14.4 6.8 copy-start.30
  15.3 19.3 %copy-start.3 = (s32[1024]{0:T(1024)S(1)}, s32[1024]{0:T(1024)}, u32[]{:S(2)}) copy-start(s32[1024]{0:T(1024)} %param.10) | copy-start | bytes 12292
  22.6 22.2 %all-to-all-start.1 = ((s32[64,4,6]{2,1,0:T(4,128)}), s32[64,4,6]{2,1,0:T(4,128)S(1)}, u32[]{:S(2)}, u32[]{:S(2)}) async-start(s32[64,4,6]{2,1,0:T(4,128)} %reshape.655), calls=%async_computation.1 | async-start | bytes 262144 | tf_op jit(solution)/shard_map/all_to_all | solution.py:156
  45.6 8.8 %all-to-all-start.2 = ((s32[4,1,384]{2,1,0:T(1,128)}), s32[4,1,384]{2,1,0:T(1,128)S(1)}, u32[]{:S(2)}, u32[]{:S(2)}) async-start(s32[4,1,384]{2,1,0:T(1,128)} %reshape.856), calls=%async_computation.2 | async-start | bytes 12288 | tf_op jit(solution)/shard_map/all_to_all | solution.py:155
  50.6 12.2 %copy-start.2 = (bf16[512,1024]{1,0:T(8,128)(2,1)S(1)}, bf16[512,1024]{1,0:T(8,128)(2,1)}, u32[]{:S(2)}) copy-start(bf16[512,1024]{1,0:T(8,128)(2,1)} %param.13) | copy-start | bytes 3145732
  54.4 34.4 %all-to-all-start = ((bf16[64,1,32,256]{3,2,1,0:T(8,128)(2,1)}), bf16[64,1,32,256]{3,2,1,0:T(8,128)(2,1)}, u32[]{:S(2)}, u32[]{:S(2)}) async-start(bf16[64,1,32,256]{3,2,1,0:T(8,128)(2,1)} %bitcast.239), calls=%async_computation | async-start | bytes 2097152 | tf_op jit(solution)/shard_map/all_to_all | solution.py:102
  62.7 5.9 copy-start.39
  88.8 79.9 %all-to-all-start.3 = ((bf16[64,4,6,1024]{3,1,2,0:T(4,128)(2,1)}), bf16[64,4,6,1024]{3,1,2,0:T(4,128)(2,1)}, u32[]{:S(2)}, u32[]{:S(2)}) async-start(bf16[64,4,6,1024]{3,1,2,0:T(4,128)(2,1)} %copy.116), calls=%async_computation.3 | async-start | bytes 6291456 | tf_op jit(solution)/shard_map/all_to_all | solution.py:165
  95.9 32.9 %all-gather.3.cloned.1.call-start = ((), (), s32[]{:S(2)}) async-start(), calls=%async_computation.8 | async-start | bytes 1310720 | tf_op jit(solution)/shard_map/all_gather | solution.py:115
  96.0 4.6 copy-start.4
  100.3 130.8 %all-reduce.8.cloned.1.call-start = ((), (), s32[]{:S(2)}) async-start(), calls=%async_computation.9 | async-start | bytes 4194304 | tf_op jit(solution)/shard_map/psum | solution.py:133
  101.2 34.4 %copy-start.47 = (f32[16]{0:T(128)}, f32[16]{0:T(128)S(1)}, u32[]{:S(2)}) copy-start(f32[16]{0:T(128)S(1)} %convert_element_type.130) | copy-start | bytes 196
  101.8 33.9 %copy-start.34 = (pred[16,32,32]{2,1,0:T(8,128)(4,1)}, pred[16,32,32]{2,1,0:T(8,128)(4,1)S(1)}, u32[]{:S(2)}) copy-start(pred[16,32,32]{2,1,0:T(8,128)(4,1)S(1)} %broadcast_and_fusion) | copy-start | bytes 49156
  128.8 3.4 copy-start.12
  130.4 4.6 copy-start.42
  136.8 4.0 copy-start.22
  173.9 60.4 %all-to-all-start.4 = ((bf16[64,4,6,1024]{3,0,2,1:T(8,128)(2,1)}), bf16[64,4,6,1024]{3,0,2,1:T(8,128)(2,1)S(1)}, u32[]{:S(2)}, u32[]{:S(2)}) async-start(bf16[64,4,6,1024]{3,0,2,1:T(8,128)(2,1)} %copy.117), calls=%async_computation.4 | async-start | bytes 6291456 | tf_op jit(solution)/shard_map/all_to_all | solution.py:164
  279.9 79.0 %all-to-all-start.5 = ((bf16[64,4,6,1024]{3,1,2,0:T(4,128)(2,1)}), bf16[64,4,6,1024]{3,1,2,0:T(4,128)(2,1)}, u32[]{:S(2)}, u32[]{:S(2)}) async-start(bf16[64,4,6,1024]{3,1,2,0:T(4,128)(2,1)} %copy.133), calls=%async_computation.6 | async-start | bytes 6291456 | tf_op jit(solution)/shard_map/all_to_all | solution.py:178
  285.7 30.1 %copy-start.15 = (bf16[256,1024]{1,0:T(8,128)(2,1)S(1)}, bf16[256,1024]{1,0:T(8,128)(2,1)}, u32[]{:S(2)}) copy-start(bf16[256,1024]{1,0:T(8,128)(2,1)} %param.15) | copy-start | bytes 1572868
  285.7 30.1 %all-gather.5.cloned.1.call-start = ((), (), s32[]{:S(2)}) async-start(), calls=%async_computation.10 | async-start | bytes 1310720 | tf_op jit(solution)/shard_map/all_gather | solution.py:195
  286.0 31.9 %copy-start.8 = (f32[16,32,2,128]{3,1,2,0:T(8,128)S(1)}, f32[16,32,2,128]{3,1,2,0:T(8,128)}, u32[]{:S(2)}) copy-start(f32[16,32,2,128]{3,1,2,0:T(8,128)} %copy-done.7) | copy-start | bytes 1572868
  286.0 31.9 %copy-start.11 = (f32[16,32,2,128]{3,2,1,0:T(2,128)S(1)}, f32[16,32,2,128]{3,2,1,0:T(2,128)}, u32[]{:S(2)}) copy-start(f32[16,32,2,128]{3,2,1,0:T(2,128)} %copy-done.10) | copy-start | bytes 1572868
  286.0 31.9 %copy-start.32 = (f32[16,32,2]{1,2,0:T(2,128)S(1)}, f32[16,32,2]{1,2,0:T(2,128)}, u32[]{:S(2)}) copy-start(f32[16,32,2]{1,2,0:T(2,128)} %get-tuple-element.29) | copy-start | bytes 12292
  286.9 31.5 %copy-start.28 = (f32[16,32,2]{1,2,0:T(2,128)S(1)}, f32[16,32,2]{1,2,0:T(2,128)}, u32[]{:S(2)}) copy-start(f32[16,32,2]{1,2,0:T(2,128)} %copy-done.27) | copy-start | bytes 12292
  286.9 31.6 %copy-start.26 = (f32[16,32,2]{1,2,0:T(2,128)S(1)}, f32[16,32,2]{1,2,0:T(2,128)}, u32[]{:S(2)}) copy-start(f32[16,32,2]{1,2,0:T(2,128)} %copy-done.25) | copy-start | bytes 12292
  286.9 251.1 %all-reduce.10.cloned.1.call-start = ((), (), s32[]{:S(2)}) async-start(), calls=%async_computation.12 | async-start | bytes 8388608
  364.3 175.2 %all-to-all-start.6 = ((bf16[64,4,6,1024]{3,0,2,1:T(8,128)(2,1)}), bf16[64,4,6,1024]{3,0,2,1:T(8,128)(2,1)S(1)}, u32[]{:S(2)}, u32[]{:S(2)}) async-start(bf16[64,4,6,1024]{3,0,2,1:T(8,128)(2,1)} %copy.134), calls=%async_computation.7 | async-start | bytes 6291456 | tf_op jit(solution)/shard_map/all_to_all | solution.py:177
  370.9 310.6 %reduce-scatter.2.cloned.1.call-start = ((), (), s32[]{:S(2)}) async-start(), calls=%async_computation.11 | async-start | bytes 1064960 | tf_op jit(solution)/shard_map/reduce_scatter | solution.py:212
  544.6 136.9 %copy-start.1 = (bf16[4,1024,256]{2,1,0:T(8,128)(2,1)S(1)}, bf16[4,1024,256]{2,1,0:T(8,128)(2,1)}, u32[]{:S(2)}) copy-start(bf16[4,1024,256]{2,1,0:T(8,128)(2,1)} %param.14) | copy-start | bytes 6291460
  (30 other events, 54.6 us)
Sparse Core Ops, SparseCore 0:
  100.4 28.3 all-gather.2
  140.9 90.1 all-reduce.7
  288.3 27.4 all-gather.4
  337.5 200.3 all-reduce.9
  542.4 139.0 reduce-scatter.1
where the time goes:
time: 695 us; the launch traced here: 688 us
  waiting for transfers between devices  423 us (61%)
  local copies, waits for them, and re-layouts  123 us (18%)
  other arithmetic  55.8 us (8%)
  starting transfers between devices  48.5 us (7%)
  matrix products  21.9 us (3%)
  between operations  15.7 us (2%)
    unnamed x6, waiting for transfers between devices  163 us
    reduce_scatter x1, waiting for transfers between devices, per_device(): lax.psum_scatter(w_out_part, 'dp', scatter_dimension=1, tiled=True)  112 us
    psum x1, waiting for transfers between devices, per_device(): summed = lax.psum(partial_out, 'mp')  34.2 us
    all_gather x1, waiting for transfers between devices, per_device(): lax.all_gather(out_grad.astype(jnp.bfloat16), 'mp', axis=0, tiled=True)  28.9 us
    all_to_all x1, waiting for transfers between devices, per_device(): lax.all_to_all(looked, 'dp', split_axis=0, concat_axis=0, tiled=True)  27.9 us
    all_gather x1, waiting for transfers between devices, per_device(): features = lax.all_gather(local_rows, 'mp', axis=2, tiled=True)  27.1 us
    all_to_all x1, waiting for transfers between devices, per_device(): lax.all_to_all(sending.reshape(dp_count, mp_count, capacity, width).astyp...  21.5 us
    scatter-add x1, other arithmetic, per_device(): cat_grad = jnp.zeros((catalogue.shape[0], width), jnp.float32).at[incomin...  16.1 us
  transfers between devices with their start and end apart: 12, of which 9 were waited for; matrix products, arithmetic and copies ran while one was open for 20% of the time, Pallas kernels for 0%

commit v1 on v0

--- a/solution.py
+++ b/solution.py
@@ -130,7 +130,7 @@
     gated_flat = gated.reshape(rows_all, cols_heads)
     partial_out = jnp.dot(gated_flat, w_out, preferred_element_type=jnp.float32)
     quarter = rows_all // mp_count
-    summed = lax.psum(partial_out, "mp")
+    summed = jnp.sum(lax.all_gather(partial_out, "mp"), axis=0)
     out_rows = lax.dynamic_slice_in_dim(summed, here_mp * quarter, quarter, 0)
     out_rows = out_rows + lax.dynamic_slice_in_dim(flat_rows, here_mp * quarter, quarter, 0).astype(
         jnp.float32

time: 695 us -> 757 us (1.089)
  blocking collectives: 0 us -> 107 us
  waiting for transfers between devices: 423 us -> 395 us
  starting transfers between devices: 48.5 us -> 29 us
    all_to_all x0 -> x3, blocking collectives: none -> 107 us  [the longest x1 77.8 us: per_device(): lax.all_to_all(looked, 'dp', split_axis=0, concat_axis=0, tiled=True)]
    psum x1 -> x0, waiting for transfers between devices: 34.2 us -> none  [per_device(): summed = lax.psum(partial_out, 'mp')]
    all_to_all x3 -> x0, waiting for transfers between devices: 32.3 us -> none  [the longest x1 27.9 us: per_device(): lax.all_to_all(looked, 'dp', split_axis=0, concat_axis=0, tiled=True)]
    all_to_all x3 -> x0, starting transfers between devices: 24 us -> none  [the longest x1 11.9 us: per_device(): lax.all_to_all(wanted, 'dp', split_axis=0, concat_axis=0, tiled=True)]
    all_to_all x1, waiting for transfers between devices: 3.51 us -> 26.2 us  [per_device(): lax.all_to_all(outgoing, 'dp', split_axis=0, concat_axis=0, tiled=True)]
    all_to_all x1, waiting for transfers between devices: 0.01 us -> 19.6 us  [per_device(): lax.all_to_all(lax.all_to_all(looked, 'dp', split_axis=0, concat_axis=0,...]
  transfers between devices with their start and end apart: 12 -> 9, of which waited for: 9 -> 7; matrix products, arithmetic and copies ran while one was open for 20% -> 18% of each run, Pallas kernels for 0% -> 0%
where the time goes in v1:
time: 757 us; the launch traced here: 746 us
  waiting for transfers between devices  395 us (52%)
  local copies, waits for them, and re-layouts  116 us (15%)
  blocking collectives  107 us (14%)
  other arithmetic  61.6 us (8%)
  starting transfers between devices  29 us (4%)
  matrix products  21.7 us (3%)
  between operations  15.7 us (2%)
    unnamed x6, waiting for transfers between devices  162 us
    reduce_scatter x1, waiting for transfers between devices, per_device(): lax.psum_scatter(w_out_part, 'dp', scatter_dimension=1, tiled=True)  112 us
    all_to_all x1, blocking collectives, per_device(): lax.all_to_all(looked, 'dp', split_axis=0, concat_axis=0, tiled=True)  77.8 us
    all_gather x1, waiting for transfers between devices, per_device(): lax.all_gather(out_grad.astype(jnp.bfloat16), 'mp', axis=0, tiled=True)  26.8 us
    all_to_all x1, waiting for transfers between devices, per_device(): lax.all_to_all(outgoing, 'dp', split_axis=0, concat_axis=0, tiled=True)  26.2 us
    all_to_all x1, waiting for transfers between devices, per_device(): lax.all_to_all(sending.reshape(dp_count, mp_count, capacity, width).astyp...  24.6 us
    all_gather x1, waiting for transfers between devices, per_device(): features = lax.all_gather(local_rows, 'mp', axis=2, tiled=True)  23.7 us
    all_to_all x1, blocking collectives, per_device(): lax.all_to_all(wanted, 'dp', split_axis=0, concat_axis=0, tiled=True)  20.5 us
  transfers between devices with their start and end apart: 9, of which 7 were waited for; matrix products, arithmetic and copies ran while one was open for 18% of the time, Pallas kernels for 0%

profile of v1, /device:TPU:8, one launch (start us, length us, event | category | flops | bytes accessed | tf_op | source)
XLA Modules:
  0.0 746.4 jit_solution(15027583963255597760)
XLA Ops:
  9.4 4.3 scatter_custom_fusion
  18.2 11.9 %all-to-all-start = ((bf16[64,1,32,256]{3,2,1,0:T(8,128)(2,1)}), bf16[64,1,32,256]{3,2,1,0:T(8,128)(2,1)S(1)}, u32[]{:S(2)}, u32[]{:S(2)}) async-start(bf16[64,1,32,256]{3,2,1,0:T(8,128)(2,1)} %bitcast.7), calls=%async_computation | async-start | bytes 2097152 | tf_op jit(solution)/shard_map/all_to_all | solution.py:102
  32.0 26.2 %all-to-all-done = bf16[64,1,32,256]{3,2,1,0:T(8,128)(2,1)S(1)} async-done(((bf16[64,1,32,256]{3,2,1,0:T(8,128)(2,1)}), bf16[64,1,32,256]{3,2,1,0:T(8,128)(2,1)S(1)}, u32[]{:S(2)}, u32[]{:S(2)}) %all-to-all-start) | async-done | bytes 1048608 | tf_op jit(solution)/shard_map/all_to_all | solution.py:102
  60.9 23.7 %all-gather.5.cloned.1.call-done = bf16[16,32,1024]{2,1,0:T(8,128)(2,1)} async-done(((bf16[16,32,256]{2,1,0:T(8,128)(2,1)}), bf16[16,32,1024]{2,1,0:T(8,128)(2,1)}) %all-gather.5.cloned.1.call-update) | async-done | bytes 1048592 | tf_op jit(solution)/shard_map/all_gather | solution.py:115
  102.6 5.9 gather_fusion.5
  109.3 20.5 %all_to_all.35 = s32[64,4,6]{2,1,0:T(4,128)S(1)} all-to-all(s32[64,4,6]{2,1,0:T(4,128)S(1)} %reshape.655), channel_id=1, replica_groups=mesh['dp'=64,'mp'=4] {'dp'}, dimensions={0} | all-to-all | bytes 12288 | tf_op jit(solution)/shard_map/all_to_all | solution.py:156
  130.0 9.1 %all_to_all.36 = s32[4,1,384]{2,1,0:T(1,128)S(1)} all-to-all(s32[4,1,384]{2,1,0:T(1,128)S(1)} %reshape.857), channel_id=1, replica_groups=mesh['dp'=64,'mp'=4] {'mp'}, dimensions={0} | all-to-all | bytes 12288 | tf_op jit(solution)/shard_map/all_to_all | solution.py:155
  140.8 5.9 gather_fusion.6
  146.7 6.3 gather.53
  155.7 6.2 copy.116
  162.0 77.8 %all_to_all.37 = bf16[64,4,6,1024]{3,1,2,0:T(4,128)(2,1)S(1)} all-to-all(bf16[64,4,6,1024]{3,1,2,0:T(4,128)(2,1)S(1)} %copy.116), channel_id=1, replica_groups=mesh['dp'=64,'mp'=4] {'dp'}, dimensions={0} | all-to-all | bytes 6291456 | tf_op jit(solution)/shard_map/all_to_all | solution.py:165
  243.2 5.4 all-to-all-start.4
  254.7 9.9 %compare_convert_fusion = f32[128]{0:T(128)S(1)} fusion(s32[]{:T(128)} %bitcast.40, s32[]{:T(128)} %bitcast.41, s32[]{:T(128)} %bitcast.42, s32[]{:T(128)} %bitcast.43, s32[]{:T(128)} %bitcast.44, s32[]{:T(128)} %bitcast.46, s32[]{:T(128)} %bitcast.45, s32[]{:T(128)} %bitcast.23, s32[]{:T(128)} %bitcast.25, s32[]{:T(128)} %bitcast.27, s32[]{:T(128)} %bitcast.29, ...), kind=kLoop, calls=%fused_computation.196 | loop fusion | flops 8064 | bytes 580 | tf_op jit(solution)/shard_map/convert_element_type | solution.py:50
  266.0 19.6 %all-to-all-done.4 = bf16[64,4,6,1024]{3,0,2,1:T(8,128)(2,1)S(1)} async-done(((bf16[64,4,6,1024]{3,0,2,1:T(8,128)(2,1)}), bf16[64,4,6,1024]{3,0,2,1:T(8,128)(2,1)S(1)}, u32[]{:S(2)}, u32[]{:S(2)}) %all-to-all-start.4) | async-done | bytes 3145760 | tf_op jit(solution)/shard_map/all_to_all | solution.py:164
  289.4 4.9 reshape.657
  294.3 5.4 gather_fusion.7
  302.2 5.9 reduce_sum.159
  318.2 5.8 gather_fusion.8
  324.0 6.2 gather.58
  330.2 4.6 fusion.1
  339.0 6.3 all-to-all-start.5
  346.6 26.8 %all-gather.7.cloned.1.call-done = bf16[512,1024]{1,0:T(8,128)(2,1)} async-done(((bf16[128,1024]{1,0:T(8,128)(2,1)}), bf16[512,1024]{1,0:T(8,128)(2,1)}) %all-gather.7.cloned.1.call-update) | async-done | bytes 1048592 | tf_op jit(solution)/shard_map/all_gather | solution.py:195
  383.7 6.1 convolution_bitcast_fusion
  389.8 5.3 copy.129
  395.0 24.6 %all-to-all-done.5 = bf16[64,4,6,1024]{3,1,2,0:T(4,128)(2,1)} async-done(((bf16[64,4,6,1024]{3,1,2,0:T(4,128)(2,1)}), bf16[64,4,6,1024]{3,1,2,0:T(4,128)(2,1)}, u32[]{:S(2)}, u32[]{:S(2)}) %all-to-all-start.5) | async-done | bytes 3145760 | tf_op jit(solution)/shard_map/all_to_all | solution.py:178
  419.7 5.3 copy.134
  425.0 5.2 all-to-all-start.6
  434.3 161.9 %all-reduce.7.cloned.1.call-done = f32[4,1024,256]{2,0,1:T(4,128)} async-done(((f32[4,1024,256]{2,0,1:T(4,128)}), f32[4,1024,256]{2,0,1:T(4,128)}) %all-reduce.7.cloned.1.call-update) | async-done | bytes 4194320
  597.7 5.1 copy.135
  602.8 8.4 %reshape.790 = f32[1536,1024]{1,0:T(8,128)} reshape(f32[64,4,6,1024]{3,2,1,0:T(8,128)} %copy.135) | data formatting | bytes 12582912 | tf_op jit(solution)/shard_map/reshape | solution.py:193
  611.3 16.1 %scatter_custom_fusion.3 = f32[512,1024]{1,0:T(8,128)} fusion(s32[1536]{0:T(1024)} %copy-done.37, f32[1536,1024]{1,0:T(8,128)} %reshape.790, f32[]{:T(128)} %constant.182.clone.1), kind=kCustom, calls=%fused_computation.68 | custom fusion | flops 1572864 | bytes 2097664 | tf_op jit(solution)/shard_map/scatter-add | solution.py:193
  627.3 112.4 %reduce-scatter.2.cloned.1.call-done = f32[256,16]{0,1:T(8,128)} async-done(((f32[256,1024]{0,1:T(8,128)}), f32[256,16]{0,1:T(8,128)}) %reduce-scatter.2.cloned.1.call-update) | async-done | bytes 16400 | tf_op jit(solution)/shard_map/reduce_scatter | solution.py:212
  (233 shorter events, 81.6 us)
Async XLA Ops:
  7.2 80.8 %copy-start = (bf16[4,1024,256]{2,1,0:T(8,128)(2,1)S(1)}, bf16[4,1024,256]{2,1,0:T(8,128)(2,1)}, u32[]{:S(2)}) copy-start(bf16[4,1024,256]{2,1,0:T(8,128)(2,1)} %param.14) | copy-start | bytes 6291460
  7.2 8.5 %copy-start.22 = (bf16[16,32,256]{2,1,0:T(8,128)(2,1)S(1)}, bf16[16,32,256]{2,1,0:T(8,128)(2,1)}, u32[]{:S(2)}) copy-start(bf16[16,32,256]{2,1,0:T(8,128)(2,1)} %param.8) | copy-start | bytes 786436
  18.2 40.1 %all-to-all-start = ((bf16[64,1,32,256]{3,2,1,0:T(8,128)(2,1)}), bf16[64,1,32,256]{3,2,1,0:T(8,128)(2,1)S(1)}, u32[]{:S(2)}, u32[]{:S(2)}) async-start(bf16[64,1,32,256]{3,2,1,0:T(8,128)(2,1)} %bitcast.7), calls=%async_computation | async-start | bytes 2097152 | tf_op jit(solution)/shard_map/all_to_all | solution.py:102
  30.1 54.5 %all-gather.5.cloned.1.call-start = ((), (), s32[]{:S(2)}) async-start(), calls=%async_computation.8 | async-start | bytes 1310720 | tf_op jit(solution)/shard_map/all_gather | solution.py:115
  30.3 29.4 %copy-start.3 = (s32[1024]{0:T(1024)S(1)}, s32[1024]{0:T(1024)}, u32[]{:S(2)}) copy-start(s32[1024]{0:T(1024)} %param.9) | copy-start | bytes 12292
  59.7 242.5 %all-gather.9.cloned.1.call-start = ((), (), s32[]{:S(2)}) async-start(), calls=%async_computation.11 | async-start | bytes 10485760 | tf_op jit(solution)/shard_map/all_gather | solution.py:133
  60.4 30.8 %copy-start.47 = (f32[16]{0:T(128)}, f32[16]{0:T(128)S(1)}, u32[]{:S(2)}) copy-start(f32[16]{0:T(128)S(1)} %convert_element_type.130) | copy-start | bytes 196
  60.9 30.2 %copy-start.33 = (pred[16,32,32]{2,1,0:T(8,128)(4,1)}, pred[16,32,32]{2,1,0:T(8,128)(4,1)S(1)}, u32[]{:S(2)}) copy-start(pred[16,32,32]{2,1,0:T(8,128)(4,1)S(1)} %broadcast_and_fusion) | copy-start | bytes 49156
  84.6 3.4 copy-start.10
  86.3 4.5 copy-start.42
  92.7 3.8 copy-start.6
  96.9 5.6 copy-start.38
  97.6 5.0 copy-start.36
  102.5 5.9 copy-start.28
  102.6 5.9 copy-start.29
  102.6 38.2 %copy-start.2 = (bf16[512,1024]{1,0:T(8,128)(2,1)S(1)}, bf16[512,1024]{1,0:T(8,128)(2,1)}, u32[]{:S(2)}) copy-start(bf16[512,1024]{1,0:T(8,128)(2,1)} %param.13) | copy-start | bytes 3145732
  140.8 5.9 copy-start.37
  243.2 42.5 %all-to-all-start.4 = ((bf16[64,4,6,1024]{3,0,2,1:T(8,128)(2,1)}), bf16[64,4,6,1024]{3,0,2,1:T(8,128)(2,1)S(1)}, u32[]{:S(2)}, u32[]{:S(2)}) async-start(bf16[64,4,6,1024]{3,0,2,1:T(8,128)(2,1)} %copy.117), calls=%async_computation.4 | async-start | bytes 6291456 | tf_op jit(solution)/shard_map/all_to_all | solution.py:164
  302.1 8.6 %copy-start.35 = (f32[128,8]{1,0:T(8,128)}, f32[128,8]{1,0:T(8,128)S(1)}, u32[]{:S(2)}) copy-start(f32[128,8]{1,0:T(8,128)S(1)} %sqrt.53) | copy-start | bytes 12292
  302.2 8.6 %copy-start.32 = (pred[128,8]{1,0:T(8,128)(4,1)S(1)}, pred[128,8]{1,0:T(8,128)(4,1)}, u32[]{:S(2)}) copy-start(pred[128,8]{1,0:T(8,128)(4,1)} %compare_and_fusion) | copy-start | bytes 3076
  339.0 80.6 %all-to-all-start.5 = ((bf16[64,4,6,1024]{3,1,2,0:T(4,128)(2,1)}), bf16[64,4,6,1024]{3,1,2,0:T(4,128)(2,1)}, u32[]{:S(2)}, u32[]{:S(2)}) async-start(bf16[64,4,6,1024]{3,1,2,0:T(4,128)(2,1)} %copy.133), calls=%async_computation.6 | async-start | bytes 6291456 | tf_op jit(solution)/shard_map/all_to_all | solution.py:178
  345.4 28.0 %copy-start.13 = (bf16[256,1024]{1,0:T(8,128)(2,1)S(1)}, bf16[256,1024]{1,0:T(8,128)(2,1)}, u32[]{:S(2)}) copy-start(bf16[256,1024]{1,0:T(8,128)(2,1)} %param.15) | copy-start | bytes 1572868
  345.4 28.0 %all-gather.7.cloned.1.call-start = ((), (), s32[]{:S(2)}) async-start(), calls=%async_computation.9 | async-start | bytes 1310720 | tf_op jit(solution)/shard_map/all_gather | solution.py:195
  345.6 29.8 %copy-start.7 = (f32[16,32,2,128]{3,1,2,0:T(8,128)S(1)}, f32[16,32,2,128]{3,1,2,0:T(8,128)}, u32[]{:S(2)}) copy-start(f32[16,32,2,128]{3,1,2,0:T(8,128)} %copy-done.6) | copy-start | bytes 1572868
  345.6 29.8 %copy-start.9 = (f32[16,32,2,128]{3,2,1,0:T(2,128)S(1)}, f32[16,32,2,128]{3,2,1,0:T(2,128)}, u32[]{:S(2)}) copy-start(f32[16,32,2,128]{3,2,1,0:T(2,128)} %copy-done.8) | copy-start | bytes 1572868
  345.6 29.8 %copy-start.31 = (f32[16,32,2]{1,2,0:T(2,128)S(1)}, f32[16,32,2]{1,2,0:T(2,128)}, u32[]{:S(2)}) copy-start(f32[16,32,2]{1,2,0:T(2,128)} %get-tuple-element.29) | copy-start | bytes 12292
  346.5 29.4 %copy-start.27 = (f32[16,32,2]{1,2,0:T(2,128)S(1)}, f32[16,32,2]{1,2,0:T(2,128)}, u32[]{:S(2)}) copy-start(f32[16,32,2]{1,2,0:T(2,128)} %copy-done.26) | copy-start | bytes 12292
  346.5 29.5 %copy-start.25 = (f32[16,32,2]{1,2,0:T(2,128)S(1)}, f32[16,32,2]{1,2,0:T(2,128)}, u32[]{:S(2)}) copy-start(f32[16,32,2]{1,2,0:T(2,128)} %copy-done.24) | copy-start | bytes 12292
  346.6 249.7 %all-reduce.7.cloned.1.call-start = ((), (), s32[]{:S(2)}) async-start(), calls=%async_computation.12 | async-start | bytes 8388608
  425.0 172.7 %all-to-all-start.6 = ((bf16[64,4,6,1024]{3,0,2,1:T(8,128)(2,1)}), bf16[64,4,6,1024]{3,0,2,1:T(8,128)(2,1)S(1)}, u32[]{:S(2)}, u32[]{:S(2)}) async-start(bf16[64,4,6,1024]{3,0,2,1:T(8,128)(2,1)} %copy.134), calls=%async_computation.7 | async-start | bytes 6291456 | tf_op jit(solution)/shard_map/all_to_all | solution.py:177
  430.2 309.5 %reduce-scatter.2.cloned.1.call-start = ((), (), s32[]{:S(2)}) async-start(), calls=%async_computation.10 | async-start | bytes 1064960 | tf_op jit(solution)/shard_map/reduce_scatter | solution.py:212
  602.8 136.9 %copy-start.1 = (bf16[4,1024,256]{2,1,0:T(8,128)(2,1)S(1)}, bf16[4,1024,256]{2,1,0:T(8,128)(2,1)}, u32[]{:S(2)}) copy-start(bf16[4,1024,256]{2,1,0:T(8,128)(2,1)} %param.14) | copy-start | bytes 6291460
  (27 other events, 47.7 us)
Sparse Core Ops, SparseCore 0:
  59.8 24.8 all-gather.4
  96.7 87.2 all-gather.8
  348.0 25.3 all-gather.6
  395.2 201.0 all-reduce.6
  600.6 139.0 reduce-scatter.1
